TPU v7x, 512 devices: a whole 4x8x8 slice. The times are simulated.
512 devices in a mesh: blk: 32 (over y_hi, x, core), chan: 16 (over z, y_lo).
Axes of the slice: x: 4, y: 8 (y_hi: 4, y_lo: 2; y = y_hi * 2 + y_lo), z: 8, core: 2. Of those that a mesh axis runs over, the one named last changes fastest.
Arguments:
- pair_repr: bfloat16 [2048, 2048, 128], P('blk', 'chan'), may hold values from -6 to 6
- chain_lengths: int32 [8], replicated, may hold values from 192 to 256
- norm_gain: float32 [128], replicated, may hold values from 0.1 to 1.9
- norm_bias: float32 [128], replicated, may hold values from -3 to 3
- left_gate: bfloat16 [128, 128], replicated, may hold values from -0.5 to 0.5
- left_value: bfloat16 [128, 128], replicated, may hold values from -0.5 to 0.5
- right_gate: bfloat16 [128, 128], replicated, may hold values from -0.5 to 0.5
- right_value: bfloat16 [128, 128], replicated, may hold values from -0.5 to 0.5
- out_gain: float32 [128], replicated, may hold values from 0.1 to 1.9
- out_bias: float32 [128], replicated, may hold values from -3 to 3
- out_weight: bfloat16 [128, 128], replicated, may hold values from -0.5 to 0.5
- gate_weight: bfloat16 [128, 128], replicated, may hold values from -0.5 to 0.5
Outputs:
- pair_update: bfloat16 [2048, 416, 128], P('blk', 'chan')
Inputs may be any that keep to these rules, and one draw needn't show every extreme that they name: Chain slot s covers residues s * 256 to (s + 1) * 256 - 1, of which the first chain_lengths[s] are real and the rest padding.
All inputs are finite; a program needn't handle non-finite values.
Results may differ from a plain program's by a relative error of at most 0.0058.
Values may be sent and summed in bfloat16 or wider, within the bound.
No kernel may reach another device: no remote copies, remote signals or barrier semaphores. Data moves between devices by JAX's collectives and lax.ppermute only.
A program may use at most 64 MiB of HBM per device.

v0:
```python
import jax
import jax.numpy as jnp
from jax import lax
from jax.sharding import PartitionSpec as P

JD = 13
epsilon = 1e-05


def normalize(values, gain_vec, bias_vec):
    centre = jnp.mean(values, axis=-1, keepdims=True)
    centred = values - centre
    spread_sq = jnp.mean(centred * centred, axis=-1, keepdims=True)
    return centred * lax.rsqrt(spread_sq + epsilon) * gain_vec + bias_vec


def residue_mask(position, lengths, slot_size):
    chain_id = position // slot_size
    chain_table = jnp.arange(lengths.shape[0], dtype=jnp.int32)
    chain_len = jnp.sum(
        jnp.where(chain_id[:, None] == chain_table[None, :], lengths[None, :], 0), axis=1
    )
    return (position % slot_size < chain_len).astype(jnp.float32)


def on_device(
    pair_repr,
    chain_lengths,
    norm_gain,
    norm_bias,
    left_gate,
    left_value,
    right_gate,
    right_value,
    out_gain,
    out_bias,
    out_weight,
    gate_weight,
):
    row_count = pair_repr.shape[0]
    col_count = pair_repr.shape[1]
    hidden = left_gate.shape[1]
    cycle_size = lax.axis_size("blk")
    cycle_index = lax.axis_index("blk")
    residues = row_count * cycle_size
    slot_size = residues // chain_lengths.shape[0]
    row_start = cycle_index * row_count
    col_start = lax.axis_index("chan") * col_count
    row_real = residue_mask(
        row_start + jnp.arange(row_count, dtype=jnp.int32), chain_lengths, slot_size
    )
    col_real = residue_mask(
        col_start + jnp.arange(col_count, dtype=jnp.int32), chain_lengths, slot_size
    )
    normed = normalize(pair_repr.astype(jnp.float32), norm_gain, norm_bias).astype(jnp.bfloat16)
    left_stack = jnp.concatenate([left_gate, left_value], axis=1)
    left_mix = jnp.einsum("ikd,de->eik", normed, left_stack, preferred_element_type=jnp.float32)
    left_proj = (
        jax.nn.sigmoid(left_mix[:hidden])
        * left_mix[hidden:]
        * (row_real[:, None] * col_real[None, :])
    ).astype(jnp.bfloat16)
    right_stack = jnp.concatenate([right_gate, right_value], axis=1)
    right_mix = jnp.einsum(
        "jkd,de->ejk", normed[:JD], right_stack, preferred_element_type=jnp.float32
    )
    right_proj = (
        jax.nn.sigmoid(right_mix[:hidden])
        * right_mix[hidden:]
        * (row_real[:JD, None] * col_real[None, :])
    ).astype(jnp.bfloat16)
    left_all, right_all = (
        lax.all_to_all(left_proj, "chan", split_axis=0, concat_axis=2, tiled=True),
        lax.all_to_all(right_proj, "chan", split_axis=0, concat_axis=2, tiled=True),
    )
    window = right_all.shape[1]
    product = jnp.einsum(
        "cik,cjk->cij",
        left_all,
        lax.all_gather(right_all, "blk", axis=1, tiled=True),
        preferred_element_type=jnp.float32,
    )
    column_slab = lax.all_to_all(
        product.astype(jnp.bfloat16), "chan", split_axis=2, concat_axis=0, tiled=True
    )
    values = column_slab.astype(jnp.float32)
    centre = jnp.mean(values, axis=0, keepdims=True)
    centred = values - centre
    spread_sq = jnp.mean(centred * centred, axis=0, keepdims=True)
    normed_product = (
        centred * lax.rsqrt(spread_sq + epsilon) * out_gain[:, None, None] + out_bias[:, None, None]
    ).astype(jnp.bfloat16)
    update = jnp.einsum(
        "cij,cd->ijd", normed_product, out_weight, preferred_element_type=jnp.float32
    )
    gate_rows = jnp.concatenate(
        [normed[:, :window], normed[:, row_count : row_count + window]], axis=1
    )
    gate_value = jax.nn.sigmoid(
        jnp.einsum("ijd,de->ije", gate_rows, gate_weight, preferred_element_type=jnp.float32)
    )
    return (gate_value * update).astype(jnp.bfloat16)


def solution(mesh):
    in_specs = (P("blk", "chan", None), P(), P(), P(), P(), P(), P(), P(), P(), P(), P(), P())
    out_specs = P("blk", "chan", None)
    return jax.shard_map(
        on_device, mesh=mesh, in_specs=in_specs, out_specs=out_specs, check_vma=False
    )
```

profile of v0, /device:TPU:2, one launch (start us, length us, event | category | flops | bytes accessed | tf_op | source)
XLA Modules:
  0.0 219.7 jit_solution(9868945080669055126)
XLA Ops:
  6.5 0.0 copy-start
  6.5 0.0 copy-start.1
  6.5 0.0 all-gather.2.cloned.1.call-start
  6.5 0.0 copy-start.8
  6.6 0.0 copy-start.9
  6.6 3.6 %convert_reduce_fusion = f32[64,128]{0,1:T(8,128)S(1)} fusion(bf16[64,128,128]{2,1,0:T(8,128)(2,1)} %param.12), kind=kLoop, calls=%fused_computation.3 | loop fusion | flops 2088960 | bytes 2129920 | tf_op jit(solution)/shard_map/reduce_sum | solution.py:11
  10.2 0.0 copy-done.1
  10.2 7.1 %fusion.4 = f32[64,128]{0,1:T(8,128)S(1)} fusion(f32[64,128]{0,1:T(8,128)S(1)} %broadcast_multiply_fusion, bf16[64,128,128]{2,1,0:T(8,128)(2,1)S(1)} %copy-done.1), kind=kLoop, calls=%fused_computation.6 | loop fusion | flops 4186112 | bytes 2162688 | tf_op jit(solution)/shard_map/reduce_sum | solution.py:13
  17.4 0.0 copy-done.11
  17.4 0.1 select_reduce_fusion
  17.5 0.1 select_reduce_fusion.1
  17.6 0.0 copy-done.8
  17.6 0.0 copy-done.9
  17.6 0.0 copy-start.4
  17.6 0.0 copy-start.5
  17.6 5.4 %fusion.7 = bf16[64,128,128]{2,0,1:T(8,128)(2,1)S(1)} fusion(f32[128]{0:T(128)S(1)} %copy-done.8, f32[128]{0:T(128)S(1)} %copy-done.9, f32[64,128]{0,1:T(8,128)S(1)} %add_rsqrt_fusion, f32[64,128]{0,1:T(8,128)S(1)} %broadcast_multiply_fusion, bf16[64,128,128]{2,1,0:T(8,128)(2,1)S(1)} %copy-done.1), kind=kLoop, calls=%fused_computation.9 | loop fusion | flops 6291456 | bytes 4260864 | tf_op jit(solution)/shard_map/convert_element_type | solution.py:55
  23.0 0.0 copy-start.2
  23.0 1.3 copy-done.2
  24.3 0.1 slice.36
  24.4 0.0 copy-done.4
  24.4 0.1 copy.59
  24.5 0.0 copy-done.5
  24.5 0.1 copy.58
  24.6 0.1 broadcast_multiply_fusion.3
  24.7 0.4 fusion.40
  25.1 0.2 fusion.29
  25.4 0.0 copy-start.6
  25.4 0.0 copy-start.7
  25.4 0.0 copy-start.3
  25.4 0.3 copy.61
  25.7 28.3 %all_to_all.45 = bf16[128,13,128]{2,1,0:T(8,128)(2,1)S(1)} all-to-all(bf16[128,13,128]{2,1,0:T(8,128)(2,1)S(1)} %copy.61), channel_id=1, replica_groups=mesh['blk'=32,'chan'=16] {'chan'}, dimensions={0} | all-to-all | bytes 851968 | tf_op jit(solution)/shard_map/all_to_all | solution.py:74
  54.0 0.3 copy.84
  54.3 0.9 all_to_all.40
  55.2 0.0 all-gather.2.cloned.1.call-update
  55.3 0.0 copy-done.6
  55.3 0.1 copy.54
  55.4 0.0 copy-done.7
  55.4 0.1 copy.53
  55.5 0.1 broadcast_multiply_fusion.1
  55.6 0.0 copy-done.3
  55.6 1.9 fusion.13
  57.5 1.2 fusion.9
  58.7 1.4 copy.56
  60.1 52.7 %all_to_all.46 = bf16[128,64,128]{2,1,0:T(8,128)(2,1)S(1)} all-to-all(bf16[128,64,128]{2,1,0:T(8,128)(2,1)S(1)} %copy.56), channel_id=1, replica_groups=mesh['blk'=32,'chan'=16] {'chan'}, dimensions={0} | all-to-all | bytes 4194304 | tf_op jit(solution)/shard_map/all_to_all | solution.py:73
  112.7 2.7 %copy.83 = bf16[16,8,64,128]{3,0,2,1:T(8,128)(2,1)} copy(bf16[16,8,64,128]{3,2,1,0:T(8,128)(2,1)S(1)} %bitcast.51) | data formatting | bytes 4194304 | tf_op jit(solution)/shard_map/all_to_all | solution.py:73
  115.5 4.2 %all_to_all.36 = bf16[8,64,2048]{2,1,0:T(8,128)(2,1)} reshape(bf16[8,64,16,128]{3,2,1,0:T(8,128)(2,1)} %bitcast.52) | data formatting | bytes 4194304 | tf_op jit(solution)/shard_map/all_to_all | solution.py:73
  119.6 44.9 %all-gather.2.cloned.1.call-done = bf16[8,416,2048]{2,0,1:T(8,128)(2,1)} async-done(((bf16[8,13,2048]{2,0,1:T(8,128)(2,1)}), bf16[8,416,2048]{2,0,1:T(8,128)(2,1)}) %all-gather.2.cloned.1.call-update) | async-done | bytes 13631504 | tf_op jit(solution)/shard_map/all_gather | solution.py:80
  164.6 20.5 %fusion.22 = bf16[8,64,416]{2,1,0:T(8,128)(2,1)S(1)} fusion(bf16[8,64,2048]{2,1,0:T(8,128)(2,1)} %all_to_all.36, bf16[8,416,2048]{2,0,1:T(8,128)(2,1)} %all-gather.2.cloned.1.call-done), kind=kOutput, calls=%fused_computation.32 | convolution fusion | flops 872628224 | bytes 16154624 | tf_op jit(solution)/shard_map/cik,cjk->cij/dot_general | solution.py:77
  185.0 0.5 copy.64
  185.5 1.3 reshape.169
  186.8 8.3 %all-to-all-start.2 = ((bf16[16,2,6656]{2,1,0:T(2,128)(2,1)}), bf16[16,2,6656]{2,1,0:T(2,128)(2,1)S(1)}, u32[]{:S(2)}, u32[]{:S(2)}) async-start(bf16[16,2,6656]{2,1,0:T(2,128)(2,1)} %reshape.169), calls=%async_computation.2 | async-start | bytes 851968 | tf_op jit(solution)/shard_map/all_to_all | solution.py:83
  195.2 0.0 copy-done
  195.2 0.4 fusion.21
  195.6 0.0 copy-start.10
  195.6 0.0 copy-start.12
  195.6 0.0 copy-start.13
  195.6 14.8 %all-to-all-done.2 = bf16[16,2,6656]{2,1,0:T(2,128)(2,1)S(1)} async-done(((bf16[16,2,6656]{2,1,0:T(2,128)(2,1)}), bf16[16,2,6656]{2,1,0:T(2,128)(2,1)S(1)}, u32[]{:S(2)}, u32[]{:S(2)}) %all-to-all-start.2) | async-done | bytes 426016 | tf_op jit(solution)/shard_map/all_to_all | solution.py:83
  210.4 0.5 reshape.170
  211.0 0.2 fusion.27
  211.2 0.3 multiply_reduce_fusion
  211.5 0.0 copy-done.10
  211.5 0.0 copy-done.12
  211.5 0.0 copy-done.13
  211.5 1.3 fusion.25
  (10 shorter events, 0.1 us)
Async XLA Ops:
  6.5 188.6 %copy-start = (bf16[128,128]{1,0:T(8,128)(2,1)S(1)}, bf16[128,128]{1,0:T(8,128)(2,1)}, u32[]{:S(2)}) copy-start(bf16[128,128]{1,0:T(8,128)(2,1)} %param.23) | copy-start | bytes 98308
  6.5 3.7 %copy-start.1 = (bf16[64,128,128]{2,1,0:T(8,128)(2,1)S(1)}, bf16[64,128,128]{2,1,0:T(8,128)(2,1)}, u32[]{:S(2)}) copy-start(bf16[64,128,128]{2,1,0:T(8,128)(2,1)} %param.12) | copy-start | bytes 6291460
  6.5 158.0 %all-gather.2.cloned.1.call-start = ((), (), s32[]{:S(2)}) async-start(), calls=%async_computation.3 | async-start | bytes 14057472 | tf_op jit(solution)/shard_map/all_gather | solution.py:80
  6.5 10.8 %copy-start.11 = (s32[8]{0:T(128)S(1)}, s32[8]{0:T(128)}, u32[]{:S(2)}) copy-start(s32[8]{0:T(128)} %param.13) | copy-start | bytes 100
  6.5 11.0 %copy-start.8 = (f32[128]{0:T(128)S(1)}, f32[128]{0:T(128)}, u32[]{:S(2)}) copy-start(f32[128]{0:T(128)} %param.15) | copy-start | bytes 1540
  6.6 11.0 %copy-start.9 = (f32[128]{0:T(128)S(1)}, f32[128]{0:T(128)}, u32[]{:S(2)}) copy-start(f32[128]{0:T(128)} %param.14) | copy-start | bytes 1540
  17.6 6.8 %copy-start.4 = (bf16[128,128]{1,0:T(8,128)(2,1)S(1)}, bf16[128,128]{1,0:T(8,128)(2,1)}, u32[]{:S(2)}) copy-start(bf16[128,128]{1,0:T(8,128)(2,1)} %param.19) | copy-start | bytes 98308
  17.6 6.9 %copy-start.5 = (bf16[128,128]{1,0:T(8,128)(2,1)S(1)}, bf16[128,128]{1,0:T(8,128)(2,1)}, u32[]{:S(2)}) copy-start(bf16[128,128]{1,0:T(8,128)(2,1)} %param.18) | copy-start | bytes 98308
  23.0 1.3 copy-start.2
  25.4 29.9 %copy-start.6 = (bf16[128,128]{1,0:T(8,128)(2,1)S(1)}, bf16[128,128]{1,0:T(8,128)(2,1)}, u32[]{:S(2)}) copy-start(bf16[128,128]{1,0:T(8,128)(2,1)} %param.17) | copy-start | bytes 98308
  25.4 30.0 %copy-start.7 = (bf16[128,128]{1,0:T(8,128)(2,1)S(1)}, bf16[128,128]{1,0:T(8,128)(2,1)}, u32[]{:S(2)}) copy-start(bf16[128,128]{1,0:T(8,128)(2,1)} %param.16) | copy-start | bytes 98308
  25.4 30.2 %copy-start.3 = (bf16[64,128,128]{2,0,1:T(8,128)(2,1)S(1)}, bf16[64,128,128]{2,0,1:T(8,128)(2,1)}, u32[]{:S(2)}) copy-start(bf16[64,128,128]{2,0,1:T(8,128)(2,1)} %copy-done.2) | copy-start | bytes 6291460
  186.8 23.6 %all-to-all-start.2 = ((bf16[16,2,6656]{2,1,0:T(2,128)(2,1)}), bf16[16,2,6656]{2,1,0:T(2,128)(2,1)S(1)}, u32[]{:S(2)}, u32[]{:S(2)}) async-start(bf16[16,2,6656]{2,1,0:T(2,128)(2,1)} %reshape.169), calls=%async_computation.2 | async-start | bytes 851968 | tf_op jit(solution)/shard_map/all_to_all | solution.py:83
  195.6 16.0 %copy-start.10 = (bf16[128,128]{1,0:T(8,128)(2,1)S(1)}, bf16[128,128]{1,0:T(8,128)(2,1)}, u32[]{:S(2)}) copy-start(bf16[128,128]{1,0:T(8,128)(2,1)} %param.22) | copy-start | bytes 98308
  195.6 16.0 %copy-start.12 = (f32[128]{0:T(128)S(1)}, f32[128]{0:T(128)}, u32[]{:S(2)}) copy-start(f32[128]{0:T(128)} %param.21) | copy-start | bytes 1540
  195.6 15.9 %copy-start.13 = (f32[128]{0:T(128)S(1)}, f32[128]{0:T(128)}, u32[]{:S(2)}) copy-start(f32[128]{0:T(128)} %param.20) | copy-start | bytes 1540
Sparse Core Ops, SparseCore 0:
  55.4 109.1 all-gather.1
where the time goes:
time: 220 us
  blocking collectives  81 us (37%)
  waiting for transfers between devices  59.8 us (27%)
  matrix products  24.4 us (11%)
  other arithmetic  18.5 us (8%)
  local copies, waits for them, and re-layouts  14 us (6%)
  between operations  13.8 us (6%)
  starting transfers between devices  8.29 us (4%)
    all_to_all x1, blocking collectives, on_device(): lax.all_to_all(left_proj, 'chan', split_axis=0, concat_axis=2, tiled=True)  52.7 us
    all_gather x1, waiting for transfers between devices, on_device(): lax.all_gather(right_all, 'blk', axis=1, tiled=True)  44.9 us
    all_to_all x1, blocking collectives, on_device(): lax.all_to_all(right_proj, 'chan', split_axis=0, concat_axis=2, tiled=True)  28.3 us
    dot_general x1, matrix products, on_device(): jnp.einsum('cik,cjk->cij', left_all, lax.all_gather(right_all, 'blk', axi...  20.5 us
    all_to_all x1, waiting for transfers between devices, on_device(): lax.all_to_all(product.astype(jnp.bfloat16), 'chan', split_axis=2, concat...  14.8 us
    all_to_all x1, starting transfers between devices, on_device(): lax.all_to_all(product.astype(jnp.bfloat16), 'chan', split_axis=2, concat...  8.29 us
    reduce_sum x1, other arithmetic, normalize(): spread_sq = jnp.mean(centred * centred, axis=-1, keepdims=True)  7.09 us
    all_to_all x2, local copies, waits for them, and re-layouts, on_device(): lax.all_to_all(left_proj, 'chan', split_axis=0, concat_axis=2, tiled=True)  6.9 us
  transfers between devices with their start and end apart: 2, of which 2 were waited for; matrix products, arithmetic and copies ran while one was open for 4% of the time, Pallas kernels for 0%

commit v1 on v0

--- a/solution.py
+++ b/solution.py
@@ -77,7 +77,9 @@
     product = jnp.einsum(
         "cik,cjk->cij",
         left_all,
-        lax.all_gather(right_all, "blk", axis=1, tiled=True),
+        jnp.concatenate(
+            lax.all_to_all(jnp.stack([right_all] * lax.axis_size("blk")), "blk", 0, 0), axis=1
+        ),
         preferred_element_type=jnp.float32,
     )
     column_slab = lax.all_to_all(

time: 220 us -> 474 us (2.15)
  the two profiles are of different devices: /device:TPU:2 before, /device:TPU:28 now
where the time goes in v1:
time: 474 us; the launch traced here: 473 us
  waiting for transfers between devices  361 us (76%)
  starting transfers between devices  44.7 us (9%)
  matrix products  24.3 us (5%)
  local copies, waits for them, and re-layouts  23.6 us (5%)
  other arithmetic  19.7 us (4%)
    all_to_all x1, waiting for transfers between devices, on_device(): lax.all_to_all(jnp.stack([right_all] * lax.axis_size('blk')), 'blk', 0, 0)  287 us
    all_to_all x1, waiting for transfers between devices, on_device(): lax.all_to_all(left_proj, 'chan', split_axis=0, concat_axis=2, tiled=True)  48.7 us
    dot_general x1, matrix products, on_device(): jnp.einsum('cik,cjk->cij', left_all, jnp.concatenate(lax.all_to_all(jnp.s...  20.4 us
    all_to_all x1, starting transfers between devices, on_device(): lax.all_to_all(product.astype(jnp.bfloat16), 'chan', split_axis=2, concat...  19.1 us
    all_to_all x1, waiting for transfers between devices, on_device(): lax.all_to_all(product.astype(jnp.bfloat16), 'chan', split_axis=2, concat...  14.1 us
    all_to_all x1, starting transfers between devices, on_device(): lax.all_to_all(right_proj, 'chan', split_axis=0, concat_axis=2, tiled=True)  11.8 us
    all_to_all x1, waiting for transfers between devices, on_device(): lax.all_to_all(right_proj, 'chan', split_axis=0, concat_axis=2, tiled=True)  10.5 us
  transfers between devices with their start and end apart: 4, of which 4 were waited for; matrix products, arithmetic and copies ran while one was open for 2% of the time, Pallas kernels for 0%

profile of v1, /device:TPU:28, one launch (start us, length us, event | category | flops | bytes accessed | tf_op | source)
XLA Modules:
  0.0 473.2 jit_solution(13356474068253222231)
XLA Ops:
  0.0 0.0 copy-start
  0.0 0.0 copy-start.1
  0.0 0.9 select_reduce_fusion.1
  0.9 0.7 select_reduce_fusion
  1.7 0.0 copy-start.9
  1.7 3.5 convert_reduce_fusion
  5.2 0.0 copy-done.1
  5.2 7.1 %fusion.4 = f32[64,128]{0,1:T(8,128)S(1)} fusion(f32[64,128]{0,1:T(8,128)S(1)} %broadcast_multiply_fusion, bf16[64,128,128]{2,1,0:T(8,128)(2,1)S(1)} %copy-done.1), kind=kLoop, calls=%fused_computation.6 | loop fusion | flops 4186112 | bytes 2162688 | tf_op jit(solution)/shard_map/reduce_sum | solution.py:13
  12.3 0.0 copy-done.8
  12.3 0.0 copy-done.9
  12.4 0.0 copy-start.4
  12.4 0.0 copy-start.5
  12.4 5.4 %fusion.7 = bf16[64,128,128]{2,0,1:T(8,128)(2,1)S(1)} fusion(f32[128]{0:T(128)S(1)} %copy-done.8, f32[128]{0:T(128)S(1)} %copy-done.9, f32[64,128]{0,1:T(8,128)S(1)} %add_rsqrt_fusion, f32[64,128]{0,1:T(8,128)S(1)} %broadcast_multiply_fusion, bf16[64,128,128]{2,1,0:T(8,128)(2,1)S(1)} %copy-done.1), kind=kLoop, calls=%fused_computation.9 | loop fusion | flops 6291456 | bytes 4260864 | tf_op jit(solution)/shard_map/convert_element_type | solution.py:55
  17.8 0.0 copy-start.2
  17.8 1.3 copy-done.2
  19.1 0.1 slice.36
  19.2 0.0 copy-done.4
  19.2 0.1 copy.57
  19.3 0.0 copy-done.5
  19.3 0.1 copy.58
  19.4 0.1 broadcast_multiply_fusion.3
  19.5 0.4 fusion.40
  19.9 0.0 copy-start.6
  19.9 0.0 copy-start.7
  19.9 0.0 copy-start.3
  19.9 0.2 fusion.29
  20.2 1.1 copy.60
  21.3 11.8 %all-to-all-start.1 = ((bf16[128,13,128]{2,1,0:T(8,128)(2,1)}), bf16[128,13,128]{2,1,0:T(8,128)(2,1)S(1)}, u32[]{:S(2)}, u32[]{:S(2)}) async-start(bf16[128,13,128]{2,1,0:T(8,128)(2,1)} %copy.60), calls=%async_computation.1 | async-start | bytes 1048576 | tf_op jit(solution)/shard_map/all_to_all | solution.py:74
  33.1 0.0 copy-done.6
  33.1 0.1 copy.52
  33.2 0.0 copy-done.7
  33.2 0.1 copy.53
  33.3 0.0 copy-done.3
  33.3 1.8 fusion.13
  35.2 0.1 broadcast_multiply_fusion.1
  35.2 1.1 fusion.9
  36.4 2.7 copy.55
  39.1 10.5 %all-to-all-done.1 = bf16[128,13,128]{2,1,0:T(8,128)(2,1)S(1)} async-done(((bf16[128,13,128]{2,1,0:T(8,128)(2,1)}), bf16[128,13,128]{2,1,0:T(8,128)(2,1)S(1)}, u32[]{:S(2)}, u32[]{:S(2)}) %all-to-all-start.1) | async-done | bytes 426016 | tf_op jit(solution)/shard_map/all_to_all | solution.py:74
  49.6 4.7 all-to-all-start
  54.2 0.3 copy.83
  54.5 0.2 stack.4
  54.7 48.7 %all-to-all-done = bf16[128,64,128]{2,1,0:T(8,128)(2,1)} async-done(((bf16[128,64,128]{2,1,0:T(8,128)(2,1)}), bf16[128,64,128]{2,1,0:T(8,128)(2,1)}, u32[]{:S(2)}, u32[]{:S(2)}) %all-to-all-start) | async-done | bytes 2097184 | tf_op jit(solution)/shard_map/all_to_all | solution.py:73
  103.4 6.6 %stack.5 = bf16[32,8,13,2048]{3,1,2,0:T(8,128)(2,1)} broadcast(bf16[8,13,2048]{2,0,1:T(8,128)(2,1)S(1)} %stack.4), dimensions={1,2,3} | broadcast | bytes 14057472 | tf_op jit(solution)/shard_map/stack | solution.py:81
  110.0 9.1 %all-to-all-start.2 = ((bf16[32,8,13,2048]{3,1,2,0:T(8,128)(2,1)}), bf16[32,8,13,2048]{3,1,2,0:T(8,128)(2,1)}, u32[]{:S(2)}, u32[]{:S(2)}) async-start(bf16[32,8,13,2048]{3,1,2,0:T(8,128)(2,1)} %stack.5), calls=%async_computation.2 | async-start | bytes 27262976 | tf_op jit(solution)/shard_map/all_to_all | solution.py:81
  119.2 4.3 copy.82
  123.5 4.2 all_to_all.37
  127.7 287.3 %all-to-all-done.2 = bf16[32,8,13,2048]{3,1,2,0:T(8,128)(2,1)} async-done(((bf16[32,8,13,2048]{3,1,2,0:T(8,128)(2,1)}), bf16[32,8,13,2048]{3,1,2,0:T(8,128)(2,1)}, u32[]{:S(2)}, u32[]{:S(2)}) %all-to-all-start.2) | async-done | bytes 13631520 | tf_op jit(solution)/shard_map/all_to_all | solution.py:81
  415.0 20.4 %fusion.22 = bf16[8,64,416]{2,1,0:T(8,128)(2,1)S(1)} fusion(bf16[8,64,2048]{2,1,0:T(8,128)(2,1)} %all_to_all.37, bf16[8,416,2048]{2,0,1:T(8,128)(2,1)} %bitcast.8), kind=kOutput, calls=%fused_computation.32 | convolution fusion | flops 872628224 | bytes 16154624 | tf_op jit(solution)/shard_map/cik,cjk->cij/dot_general | solution.py:77
  435.4 0.5 copy.63
  435.9 1.3 reshape.180
  437.2 19.1 %all-to-all-start.3 = ((bf16[16,2,6656]{2,1,0:T(2,128)(2,1)}), bf16[16,2,6656]{2,1,0:T(2,128)(2,1)S(1)}, u32[]{:S(2)}, u32[]{:S(2)}) async-start(bf16[16,2,6656]{2,1,0:T(2,128)(2,1)} %reshape.180), calls=%async_computation.3 | async-start | bytes 851968 | tf_op jit(solution)/shard_map/all_to_all | solution.py:85
  456.4 0.0 copy-done
  456.4 0.4 fusion.21
  456.7 0.0 copy-start.10
  456.8 0.0 copy-start.11
  456.8 0.0 copy-start.12
  456.8 14.1 %all-to-all-done.3 = bf16[16,2,6656]{2,1,0:T(2,128)(2,1)S(1)} async-done(((bf16[16,2,6656]{2,1,0:T(2,128)(2,1)}), bf16[16,2,6656]{2,1,0:T(2,128)(2,1)S(1)}, u32[]{:S(2)}, u32[]{:S(2)}) %all-to-all-start.3) | async-done | bytes 426016 | tf_op jit(solution)/shard_map/all_to_all | solution.py:85
  470.9 0.5 reshape.181
  471.4 0.2 fusion.27
  471.6 0.3 multiply_reduce_fusion
  471.9 0.0 copy-done.10
  472.0 0.0 copy-done.11
  472.0 0.0 copy-done.12
  472.0 1.3 fusion.25
  (10 shorter events, 0.1 us)
Async XLA Ops:
  0.0 456.4 %copy-start = (bf16[128,128]{1,0:T(8,128)(2,1)S(1)}, bf16[128,128]{1,0:T(8,128)(2,1)}, u32[]{:S(2)}) copy-start(bf16[128,128]{1,0:T(8,128)(2,1)} %param.23) | copy-start | bytes 98308
  0.0 5.2 %copy-start.1 = (bf16[64,128,128]{2,1,0:T(8,128)(2,1)S(1)}, bf16[64,128,128]{2,1,0:T(8,128)(2,1)}, u32[]{:S(2)}) copy-start(bf16[64,128,128]{2,1,0:T(8,128)(2,1)} %param.12) | copy-start | bytes 6291460
  1.7 10.7 %copy-start.8 = (f32[128]{0:T(128)S(1)}, f32[128]{0:T(128)}, u32[]{:S(2)}) copy-start(f32[128]{0:T(128)} %param.15) | copy-start | bytes 1540
  1.7 10.7 %copy-start.9 = (f32[128]{0:T(128)S(1)}, f32[128]{0:T(128)}, u32[]{:S(2)}) copy-start(f32[128]{0:T(128)} %param.14) | copy-start | bytes 1540
  12.4 6.8 %copy-start.4 = (bf16[128,128]{1,0:T(8,128)(2,1)S(1)}, bf16[128,128]{1,0:T(8,128)(2,1)}, u32[]{:S(2)}) copy-start(bf16[128,128]{1,0:T(8,128)(2,1)} %param.18) | copy-start | bytes 98308
  12.4 6.9 %copy-start.5 = (bf16[128,128]{1,0:T(8,128)(2,1)S(1)}, bf16[128,128]{1,0:T(8,128)(2,1)}, u32[]{:S(2)}) copy-start(bf16[128,128]{1,0:T(8,128)(2,1)} %param.19) | copy-start | bytes 98308
  17.8 1.3 copy-start.2
  19.9 13.1 %copy-start.6 = (bf16[128,128]{1,0:T(8,128)(2,1)S(1)}, bf16[128,128]{1,0:T(8,128)(2,1)}, u32[]{:S(2)}) copy-start(bf16[128,128]{1,0:T(8,128)(2,1)} %param.16) | copy-start | bytes 98308
  19.9 13.3 %copy-start.7 = (bf16[128,128]{1,0:T(8,128)(2,1)S(1)}, bf16[128,128]{1,0:T(8,128)(2,1)}, u32[]{:S(2)}) copy-start(bf16[128,128]{1,0:T(8,128)(2,1)} %param.17) | copy-start | bytes 98308
  19.9 13.4 %copy-start.3 = (bf16[64,128,128]{2,0,1:T(8,128)(2,1)S(1)}, bf16[64,128,128]{2,0,1:T(8,128)(2,1)}, u32[]{:S(2)}) copy-start(bf16[64,128,128]{2,0,1:T(8,128)(2,1)} %copy-done.2) | copy-start | bytes 6291460
  21.3 28.3 %all-to-all-start.1 = ((bf16[128,13,128]{2,1,0:T(8,128)(2,1)}), bf16[128,13,128]{2,1,0:T(8,128)(2,1)S(1)}, u32[]{:S(2)}, u32[]{:S(2)}) async-start(bf16[128,13,128]{2,1,0:T(8,128)(2,1)} %copy.60), calls=%async_computation.1 | async-start | bytes 1048576 | tf_op jit(solution)/shard_map/all_to_all | solution.py:74
  49.6 53.8 %all-to-all-start = ((bf16[128,64,128]{2,1,0:T(8,128)(2,1)}), bf16[128,64,128]{2,1,0:T(8,128)(2,1)}, u32[]{:S(2)}, u32[]{:S(2)}) async-start(bf16[128,64,128]{2,1,0:T(8,128)(2,1)} %copy.55), calls=%async_computation | async-start | bytes 4194304 | tf_op jit(solution)/shard_map/all_to_all | solution.py:73
  110.0 305.0 %all-to-all-start.2 = ((bf16[32,8,13,2048]{3,1,2,0:T(8,128)(2,1)}), bf16[32,8,13,2048]{3,1,2,0:T(8,128)(2,1)}, u32[]{:S(2)}, u32[]{:S(2)}) async-start(bf16[32,8,13,2048]{3,1,2,0:T(8,128)(2,1)} %stack.5), calls=%async_computation.2 | async-start | bytes 27262976 | tf_op jit(solution)/shard_map/all_to_all | solution.py:81
  437.2 33.7 %all-to-all-start.3 = ((bf16[16,2,6656]{2,1,0:T(2,128)(2,1)}), bf16[16,2,6656]{2,1,0:T(2,128)(2,1)S(1)}, u32[]{:S(2)}, u32[]{:S(2)}) async-start(bf16[16,2,6656]{2,1,0:T(2,128)(2,1)} %reshape.180), calls=%async_computation.3 | async-start | bytes 851968 | tf_op jit(solution)/shard_map/all_to_all | solution.py:85
  456.7 15.2 %copy-start.10 = (bf16[128,128]{1,0:T(8,128)(2,1)S(1)}, bf16[128,128]{1,0:T(8,128)(2,1)}, u32[]{:S(2)}) copy-start(bf16[128,128]{1,0:T(8,128)(2,1)} %param.22) | copy-start | bytes 98308
  456.8 15.2 %copy-start.11 = (f32[128]{0:T(128)S(1)}, f32[128]{0:T(128)}, u32[]{:S(2)}) copy-start(f32[128]{0:T(128)} %param.21) | copy-start | bytes 1540
  456.8 15.2 %copy-start.12 = (f32[128]{0:T(128)S(1)}, f32[128]{0:T(128)}, u32[]{:S(2)}) copy-start(f32[128]{0:T(128)} %param.20) | copy-start | bytes 1540
